TPU v7x, 128 devices: a whole 4x4x4 slice. The times are simulated.
128 devices in a mesh: seq: 32 (over x, y, core), head: 4 (over z).
Axes of the slice: x: 4, y: 4, z: 4, core: 2. Of those that a mesh axis runs over, the one named last changes fastest.
Arguments:
- queries: bfloat16 [65536, 4096], P('seq', 'head'), may hold values from -2 to 2
- key_rows: bfloat16 [65536, 4096], P('seq', 'head'), may hold values from -2 to 2
- value_rows: bfloat16 [65536, 4096], P('seq', 'head'), may hold values from -128 to 128
- decay_log: float32 [32, 65536], P('head', 'seq'), may hold values from -0.8 to 0
- norm_gain: float32 [4096], P('head'), may hold values from 0.1 to 1.9
- page_owner: int32 [64], replicated, may hold values from 0 to 31, as said below
Outputs:
- attended: bfloat16 [65536, 4096], P('seq', 'head')
- page_cache: bfloat16 [160, 32, 128, 128], P('seq', 'head')
Inputs may be any that keep to these rules, and one draw needn't show every extreme that they name: `page_owner`: the 2 pages p = i * 2 to (i + 1) * 2 - 1 have different owners for every i; no owner keeps more than 5 pages and one keeps exactly 5.
All inputs are finite; a program needn't handle non-finite values.
Results may differ from a plain program's by a relative error of at most 0.0042.
Values may be sent and summed in bfloat16 or wider, within the bound.
A program may use at most 128 MiB of HBM per device.

v0:
```python
import jax
import jax.numpy as jnp
from jax import lax
from jax.sharding import PartitionSpec as P

BLOCK = 512
PAGE = 1024
SLOTS = 5


def from_behind(value, axis, steps):
    count = lax.axis_size(axis)
    first, last = (max(0, -steps), min(count, count - steps))
    return lax.ppermute(value, axis, [(source, source + steps) for source in range(first, last)])


def block_terms(query_blk, key_blk, value_blk, cumulative, carry_state):
    length = cumulative.shape[1]
    token_positions = jnp.arange(length)
    causal = (token_positions[:, None] >= token_positions[None, :])[None]
    spread = cumulative[:, :, None] - cumulative[:, None, :]
    damping = jnp.where(causal, jnp.exp(jnp.where(causal, spread, 0.0)), 0.0)
    scores = jnp.einsum("thd,shd->hts", query_blk, key_blk, preferred_element_type=jnp.float32)
    weights = (scores * damping).astype(jnp.bfloat16)
    inner_sum = jnp.einsum("hts,shd->thd", weights, value_blk, preferred_element_type=jnp.float32)
    carried = jnp.einsum(
        "thd,hde->the", query_blk.astype(jnp.float32), carry_state, precision=lax.Precision.HIGHEST
    )
    output = inner_sum + carried * jnp.exp(cumulative).T[:, :, None]
    scaled_keys = (
        key_blk.astype(jnp.float32) * jnp.exp(cumulative[:, -1:] - cumulative).T[:, :, None]
    ).astype(jnp.bfloat16)
    update = jnp.einsum("shd,she->hde", scaled_keys, value_blk, preferred_element_type=jnp.float32)
    new_state = jnp.exp(cumulative[:, -1])[:, None, None] * carry_state + update
    return (output, new_state)


def combine(earlier, following):
    return (
        earlier[0] + following[0],
        jnp.exp(following[0])[:, None, None] * earlier[1] + following[1],
    )


def shards(queries, key_rows, value_rows, decay_log, norm_gain, page_owner):
    tok_rows, width_dev = queries.shape
    head_count = decay_log.shape[0]
    head_dim = width_dev // head_count
    block_count = tok_rows // BLOCK
    grid_shape = (block_count, BLOCK, head_count, head_dim)
    query_blocks = queries.reshape(grid_shape)
    key_blocks = key_rows.reshape(grid_shape)
    value_blocks = value_rows.reshape(grid_shape)
    cumulative = jnp.cumsum(decay_log.reshape(head_count, block_count, BLOCK), axis=2)
    block_decay = cumulative[:, :, -1]
    reached = jnp.cumsum(block_decay, axis=1)

    def local_step(carry_state, pieces):
        query_blk, key_blk, value_blk, decay_blk = pieces
        output, new_state = block_terms(query_blk, key_blk, value_blk, decay_blk, carry_state)
        return (new_state, (output, new_state))

    zero_state = jnp.zeros((head_count, head_dim, head_dim), jnp.float32)
    local_end, (local_out, block_states) = lax.scan(
        local_step,
        zero_state,
        (query_blocks, key_blocks, value_blocks, cumulative.transpose(1, 0, 2)),
    )
    own_part = (reached[:, -1], local_end)
    identity = (jnp.zeros((head_count,), jnp.float32), zero_state)

    def relay_turn(turn_index, incoming):
        return from_behind(combine(incoming, own_part), "seq", 1)

    incoming = lax.fori_loop(0, lax.axis_size("seq") - 1, relay_turn, identity)
    entry_state = incoming[1]
    start_log = reached - block_decay
    total_log = (cumulative + start_log[:, :, None]).reshape(head_count, tok_rows).T
    entry_term = jnp.einsum(
        "thd,hde->the",
        queries.reshape(tok_rows, head_count, head_dim).astype(jnp.float32),
        entry_state,
        precision=lax.Precision.HIGHEST,
    )
    output = (
        local_out.reshape(tok_rows, head_count, head_dim)
        + entry_term * jnp.exp(total_log)[:, :, None]
    )
    square_sum = jnp.sum(output * output, axis=(1, 2))
    total_square = lax.psum(square_sum, "head")
    scale_row = lax.rsqrt(total_square / (head_count * head_dim * lax.axis_size("head")) + 1e-06)
    normed = output * scale_row[:, None, None] * norm_gain.reshape(head_count, head_dim)[None]
    attended = normed.astype(jnp.bfloat16).reshape(tok_rows, width_dev)
    per_page = PAGE // BLOCK
    page_decay = jnp.exp(reached[:, per_page - 1 :: per_page]).T
    snapshots = (
        page_decay[:, :, None, None] * entry_state[None] + block_states[per_page - 1 :: per_page]
    ).astype(jnp.bfloat16)
    page_order = jnp.arange(page_owner.shape[0])
    earlier = (page_owner[:, None] == page_owner[None, :]) & (
        page_order[None, :] < page_order[:, None]
    )
    slot_index = jnp.sum(earlier.astype(jnp.int32), axis=1)
    seq_index = lax.axis_index("seq")
    slot_ids = jnp.arange(SLOTS)
    chosen = (page_owner[None, :] == seq_index) & (slot_index[None, :] == slot_ids[:, None])
    gathered = jnp.einsum(
        "sn,nhde->shde",
        chosen.astype(jnp.bfloat16),
        lax.all_gather(snapshots, "seq", axis=0, tiled=True),
        preferred_element_type=jnp.float32,
    )
    page_cache = gathered.astype(jnp.bfloat16)
    return (attended, page_cache)


def solution(mesh):
    return jax.shard_map(
        shards,
        mesh=mesh,
        in_specs=(
            P("seq", "head"),
            P("seq", "head"),
            P("seq", "head"),
            P("head", "seq"),
            P("head"),
            P(),
        ),
        out_specs=(P("seq", "head"), P("seq", "head", None, None)),
        check_vma=False,
    )
```

profile of v0, /device:TPU:1, one launch (start us, length us, event | category | flops | bytes accessed | tf_op | source)
XLA Modules:
  0.0 800.7 jit_solution(18202910825025236144)
XLA Ops:
  27.2 248.2 %while.28 = (s32[]{:T(128)}, f32[8,128,128]{2,1,0:T(8,128)}, f32[4,512,8,128]{1,0,3,2:T(4,128)}, f32[4,8,128,128]{3,2,1,0:T(8,128)}, f32[4,8,512]{2,1,0:T(8,128)...) while((s32[]{:T(128)}, f32[8,128,128]{2,1,0:T(8,128)}, ...), condition=%wide.region_3.4_spmd.clone, body=%wide.region_2.3_spmd.clone.sunk | while | flops 2027163648 | bytes 38535560 | solution.py:64
  48.1 41.0 %dynamic_update_slice.14 = f32[4,512,8,128]{1,0,3,2:T(4,128)} dynamic-update-slice(f32[4,512,8,128]{1,0,3,2:T(4,128)} %get-tuple-element.309, f32[1,512,8,128]{1,0,3,2:T(1,128)} %copy.188, s32[]{:T(128)S(6)} %copy.195, s32[]{:T(128)} %constant.44.clone.1..sunk, s32[]{:T(128)} %constant.44.clone.1..sunk, s32[]{:T(128)} %constant.44.clone.1..sunk) | dynamic-update-slice | bytes 4194308 | tf_op jit(solution)/shard_map/while/body/jit(dynamic_update_index_in_dim)/dynamic_update_slice | solution.py:64
  110.2 41.0 %dynamic_update_slice.14 = f32[4,512,8,128]{1,0,3,2:T(4,128)} dynamic-update-slice(f32[4,512,8,128]{1,0,3,2:T(4,128)} %get-tuple-element.309, f32[1,512,8,128]{1,0,3,2:T(1,128)} %copy.188, s32[]{:T(128)S(6)} %copy.195, s32[]{:T(128)} %constant.44.clone.1..sunk, s32[]{:T(128)} %constant.44.clone.1..sunk, s32[]{:T(128)} %constant.44.clone.1..sunk) | dynamic-update-slice | bytes 4194308 | tf_op jit(solution)/shard_map/while/body/jit(dynamic_update_index_in_dim)/dynamic_update_slice | solution.py:64
  172.3 41.0 %dynamic_update_slice.14 = f32[4,512,8,128]{1,0,3,2:T(4,128)} dynamic-update-slice(f32[4,512,8,128]{1,0,3,2:T(4,128)} %get-tuple-element.309, f32[1,512,8,128]{1,0,3,2:T(1,128)} %copy.188, s32[]{:T(128)S(6)} %copy.195, s32[]{:T(128)} %constant.44.clone.1..sunk, s32[]{:T(128)} %constant.44.clone.1..sunk, s32[]{:T(128)} %constant.44.clone.1..sunk) | dynamic-update-slice | bytes 4194308 | tf_op jit(solution)/shard_map/while/body/jit(dynamic_update_index_in_dim)/dynamic_update_slice | solution.py:64
  234.4 41.0 %dynamic_update_slice.14 = f32[4,512,8,128]{1,0,3,2:T(4,128)} dynamic-update-slice(f32[4,512,8,128]{1,0,3,2:T(4,128)} %get-tuple-element.309, f32[1,512,8,128]{1,0,3,2:T(1,128)} %copy.188, s32[]{:T(128)S(6)} %copy.195, s32[]{:T(128)} %constant.44.clone.1..sunk, s32[]{:T(128)} %constant.44.clone.1..sunk, s32[]{:T(128)} %constant.44.clone.1..sunk) | dynamic-update-slice | bytes 4194308 | tf_op jit(solution)/shard_map/while/body/jit(dynamic_update_index_in_dim)/dynamic_update_slice | solution.py:64
  276.1 388.3 %while.27 = (s32[]{:T(128)}, f32[8,128,128]{2,1,0:T(8,128)S(1)}, f32[8,1,1]{0,2,1:T(1,128)}, f32[8,128,128]{2,1,0:T(8,128)}, s32[]{:T(128)}) while((s32[]{:T(128)}, f32[8,128,128]{2,1,0:T(8,128)S(1)}, f32[8,1,1]{0,2,1:T(1,128)}, f32[8,128,128]{2,1,0:T(8,128)}, s32[]{:T(128)}) %tuple.70), condition=%wide.region_6.7_spmd, body=%wide.region_5.6_spmd.sunk | while | flops 262146 | bytes 3670149 | solution.py:75
  500.3 6.5 collective-permute-start
  514.0 6.5 collective-permute-start
  527.8 6.5 collective-permute-start
  541.6 6.5 collective-permute-start
  555.4 6.5 collective-permute-start
  569.1 6.5 collective-permute-start
  582.9 6.5 collective-permute-start
  596.7 6.5 collective-permute-start
  610.4 6.5 collective-permute-start
  624.2 6.5 collective-permute-start
  638.0 6.5 collective-permute-start
  651.8 6.5 collective-permute-start
  665.4 10.9 %reshape.92 = f32[2048,8,128]{0,2,1:T(8,128)} reshape(f32[4,512,8,128]{1,0,3,2:T(4,128)} %get-tuple-element.96) | data formatting | bytes 16777216 | tf_op jit(solution)/shard_map/reshape | solution.py:86
  677.5 12.3 %multiply_reduce_fusion = (f32[2048]{0:T(1024)S(1)}, f32[2048,8,128]{0,2,1:T(8,128)}) fusion(f32[2048,8,128]{0,2,1:T(8,128)} %reshape.92, f32[2048,8]{0,1:T(8,128)S(1)} %exponential_bitcast_fusion.2, f32[8,128,128]{2,1,0:T(8,128)S(1)} %get-tuple-element.98, bf16[2048,1024]{1,0:T(8,128)(2,1)} %param.10), kind=kOutput, calls=%fused_computation.34 | convolution fusion | flops 3229612032 | bytes 21569536 | tf_op jit(solution)/shard_map/thd,hde->the/dot_general | solution.py:79
  689.8 9.8 %psum.7 = f32[2048]{0:T(1024)S(1)} all-reduce(f32[2048]{0:T(1024)S(1)} %get-tuple-element.209), channel_id=1, replica_groups=mesh['seq'=32,'head'=4] {'head'}, use_global_device_ids=true, to_apply=%region_8.9 | all-reduce | flops 2048 | bytes 16384 | tf_op jit(solution)/shard_map/psum | solution.py:90
  705.7 6.4 copy.116
  712.3 65.4 %all-gather.2.cloned.1.call-done = bf16[64,8,128,128]{3,2,1,0:T(8,128)(2,1)} async-done(((bf16[2,8,128,128]{3,2,1,0:T(8,128)(2,1)}), bf16[64,8,128,128]{3,2,1,0:T(8,128)(2,1)}) %all-gather.2.cloned.1.call-update) | async-done | bytes 16777232 | tf_op jit(solution)/shard_map/all_gather | solution.py:110
  777.7 14.7 %fusion.18 = bf16[5,8,128,128]{3,0,2,1:T(8,128)(2,1)S(1)} fusion(bf16[64,8,128,128]{3,2,1,0:T(8,128)(2,1)} %all-gather.2.cloned.1.call-done, s32[64]{0:T(128)S(1)} %convert_reduce_fusion, pred[64]{0:T(512)(128)(4,1)S(1)} %broadcast_compare_fusion), kind=kOutput, calls=%fused_computation.37 | convolution fusion | flops 84542080 | bytes 18088256 | tf_op jit(solution)/shard_map/sn,nhde->shde/dot_general | solution.py:107
  (211 shorter events, 424.4 us)
Async XLA Ops:
  7.2 770.6 %all-gather.2.cloned.1.call-start = ((), (), s32[]{:S(2)}) async-start(), calls=%async_computation | async-start | bytes 17301504 | tf_op jit(solution)/shard_map/all_gather | solution.py:110
  277.4 10.7 %collective-permute-start = (f32[8,128,128]{2,1,0:T(8,128)S(1)}, f32[8,128,128]{2,1,0:T(8,128)S(1)}, u32[]{:S(2)}, u32[]{:S(2)}) collective-permute-start(f32[8,128,128]{2,1,0:T(8,128)S(1)} %multiply_add_fusion.2), channel_id=1, source_target_pairs={{0,4},{4,8},{8,12},{12,16},{16,20},{20,24},{24,28},{28,32},{32,36}... | collective-permute-start | bytes 1572872 | tf_op jit(solution)/shard_map/while/body/eval_jaxpr/ppermute | solution.py:14
  289.3 10.5 %collective-permute-start = (f32[8,128,128]{2,1,0:T(8,128)S(1)}, f32[8,128,128]{2,1,0:T(8,128)S(1)}, u32[]{:S(2)}, u32[]{:S(2)}) collective-permute-start(f32[8,128,128]{2,1,0:T(8,128)S(1)} %multiply_add_fusion.2), channel_id=1, source_target_pairs={{0,4},{4,8},{8,12},{12,16},{16,20},{20,24},{24,28},{28,32},{32,36}... | collective-permute-start | bytes 1572872 | tf_op jit(solution)/shard_map/while/body/eval_jaxpr/ppermute | solution.py:14
  300.9 10.5 %collective-permute-start = (f32[8,128,128]{2,1,0:T(8,128)S(1)}, f32[8,128,128]{2,1,0:T(8,128)S(1)}, u32[]{:S(2)}, u32[]{:S(2)}) collective-permute-start(f32[8,128,128]{2,1,0:T(8,128)S(1)} %multiply_add_fusion.2), channel_id=1, source_target_pairs={{0,4},{4,8},{8,12},{12,16},{16,20},{20,24},{24,28},{28,32},{32,36}... | collective-permute-start | bytes 1572872 | tf_op jit(solution)/shard_map/while/body/eval_jaxpr/ppermute | solution.py:14
  312.6 10.5 %collective-permute-start = (f32[8,128,128]{2,1,0:T(8,128)S(1)}, f32[8,128,128]{2,1,0:T(8,128)S(1)}, u32[]{:S(2)}, u32[]{:S(2)}) collective-permute-start(f32[8,128,128]{2,1,0:T(8,128)S(1)} %multiply_add_fusion.2), channel_id=1, source_target_pairs={{0,4},{4,8},{8,12},{12,16},{16,20},{20,24},{24,28},{28,32},{32,36}... | collective-permute-start | bytes 1572872 | tf_op jit(solution)/shard_map/while/body/eval_jaxpr/ppermute | solution.py:14
  324.3 10.5 %collective-permute-start = (f32[8,128,128]{2,1,0:T(8,128)S(1)}, f32[8,128,128]{2,1,0:T(8,128)S(1)}, u32[]{:S(2)}, u32[]{:S(2)}) collective-permute-start(f32[8,128,128]{2,1,0:T(8,128)S(1)} %multiply_add_fusion.2), channel_id=1, source_target_pairs={{0,4},{4,8},{8,12},{12,16},{16,20},{20,24},{24,28},{28,32},{32,36}... | collective-permute-start | bytes 1572872 | tf_op jit(solution)/shard_map/while/body/eval_jaxpr/ppermute | solution.py:14
  347.6 10.5 %collective-permute-start = (f32[8,128,128]{2,1,0:T(8,128)S(1)}, f32[8,128,128]{2,1,0:T(8,128)S(1)}, u32[]{:S(2)}, u32[]{:S(2)}) collective-permute-start(f32[8,128,128]{2,1,0:T(8,128)S(1)} %multiply_add_fusion.2), channel_id=1, source_target_pairs={{0,4},{4,8},{8,12},{12,16},{16,20},{20,24},{24,28},{28,32},{32,36}... | collective-permute-start | bytes 1572872 | tf_op jit(solution)/shard_map/while/body/eval_jaxpr/ppermute | solution.py:14
  370.9 10.5 %collective-permute-start = (f32[8,128,128]{2,1,0:T(8,128)S(1)}, f32[8,128,128]{2,1,0:T(8,128)S(1)}, u32[]{:S(2)}, u32[]{:S(2)}) collective-permute-start(f32[8,128,128]{2,1,0:T(8,128)S(1)} %multiply_add_fusion.2), channel_id=1, source_target_pairs={{0,4},{4,8},{8,12},{12,16},{16,20},{20,24},{24,28},{28,32},{32,36}... | collective-permute-start | bytes 1572872 | tf_op jit(solution)/shard_map/while/body/eval_jaxpr/ppermute | solution.py:14
  394.3 10.5 %collective-permute-start = (f32[8,128,128]{2,1,0:T(8,128)S(1)}, f32[8,128,128]{2,1,0:T(8,128)S(1)}, u32[]{:S(2)}, u32[]{:S(2)}) collective-permute-start(f32[8,128,128]{2,1,0:T(8,128)S(1)} %multiply_add_fusion.2), channel_id=1, source_target_pairs={{0,4},{4,8},{8,12},{12,16},{16,20},{20,24},{24,28},{28,32},{32,36}... | collective-permute-start | bytes 1572872 | tf_op jit(solution)/shard_map/while/body/eval_jaxpr/ppermute | solution.py:14
  417.6 10.5 %collective-permute-start = (f32[8,128,128]{2,1,0:T(8,128)S(1)}, f32[8,128,128]{2,1,0:T(8,128)S(1)}, u32[]{:S(2)}, u32[]{:S(2)}) collective-permute-start(f32[8,128,128]{2,1,0:T(8,128)S(1)} %multiply_add_fusion.2), channel_id=1, source_target_pairs={{0,4},{4,8},{8,12},{12,16},{16,20},{20,24},{24,28},{28,32},{32,36}... | collective-permute-start | bytes 1572872 | tf_op jit(solution)/shard_map/while/body/eval_jaxpr/ppermute | solution.py:14
  440.9 10.5 %collective-permute-start = (f32[8,128,128]{2,1,0:T(8,128)S(1)}, f32[8,128,128]{2,1,0:T(8,128)S(1)}, u32[]{:S(2)}, u32[]{:S(2)}) collective-permute-start(f32[8,128,128]{2,1,0:T(8,128)S(1)} %multiply_add_fusion.2), channel_id=1, source_target_pairs={{0,4},{4,8},{8,12},{12,16},{16,20},{20,24},{24,28},{28,32},{32,36}... | collective-permute-start | bytes 1572872 | tf_op jit(solution)/shard_map/while/body/eval_jaxpr/ppermute | solution.py:14
  487.6 11.5 %collective-permute-start = (f32[8,128,128]{2,1,0:T(8,128)S(1)}, f32[8,128,128]{2,1,0:T(8,128)S(1)}, u32[]{:S(2)}, u32[]{:S(2)}) collective-permute-start(f32[8,128,128]{2,1,0:T(8,128)S(1)} %multiply_add_fusion.2), channel_id=1, source_target_pairs={{0,4},{4,8},{8,12},{12,16},{16,20},{20,24},{24,28},{28,32},{32,36}... | collective-permute-start | bytes 1572872 | tf_op jit(solution)/shard_map/while/body/eval_jaxpr/ppermute | solution.py:14
  500.3 12.6 %collective-permute-start = (f32[8,128,128]{2,1,0:T(8,128)S(1)}, f32[8,128,128]{2,1,0:T(8,128)S(1)}, u32[]{:S(2)}, u32[]{:S(2)}) collective-permute-start(f32[8,128,128]{2,1,0:T(8,128)S(1)} %multiply_add_fusion.2), channel_id=1, source_target_pairs={{0,4},{4,8},{8,12},{12,16},{16,20},{20,24},{24,28},{28,32},{32,36}... | collective-permute-start | bytes 1572872 | tf_op jit(solution)/shard_map/while/body/eval_jaxpr/ppermute | solution.py:14
  514.0 12.6 %collective-permute-start = (f32[8,128,128]{2,1,0:T(8,128)S(1)}, f32[8,128,128]{2,1,0:T(8,128)S(1)}, u32[]{:S(2)}, u32[]{:S(2)}) collective-permute-start(f32[8,128,128]{2,1,0:T(8,128)S(1)} %multiply_add_fusion.2), channel_id=1, source_target_pairs={{0,4},{4,8},{8,12},{12,16},{16,20},{20,24},{24,28},{28,32},{32,36}... | collective-permute-start | bytes 1572872 | tf_op jit(solution)/shard_map/while/body/eval_jaxpr/ppermute | solution.py:14
  527.8 12.6 %collective-permute-start = (f32[8,128,128]{2,1,0:T(8,128)S(1)}, f32[8,128,128]{2,1,0:T(8,128)S(1)}, u32[]{:S(2)}, u32[]{:S(2)}) collective-permute-start(f32[8,128,128]{2,1,0:T(8,128)S(1)} %multiply_add_fusion.2), channel_id=1, source_target_pairs={{0,4},{4,8},{8,12},{12,16},{16,20},{20,24},{24,28},{28,32},{32,36}... | collective-permute-start | bytes 1572872 | tf_op jit(solution)/shard_map/while/body/eval_jaxpr/ppermute | solution.py:14
  541.6 12.6 %collective-permute-start = (f32[8,128,128]{2,1,0:T(8,128)S(1)}, f32[8,128,128]{2,1,0:T(8,128)S(1)}, u32[]{:S(2)}, u32[]{:S(2)}) collective-permute-start(f32[8,128,128]{2,1,0:T(8,128)S(1)} %multiply_add_fusion.2), channel_id=1, source_target_pairs={{0,4},{4,8},{8,12},{12,16},{16,20},{20,24},{24,28},{28,32},{32,36}... | collective-permute-start | bytes 1572872 | tf_op jit(solution)/shard_map/while/body/eval_jaxpr/ppermute | solution.py:14
  555.4 12.6 %collective-permute-start = (f32[8,128,128]{2,1,0:T(8,128)S(1)}, f32[8,128,128]{2,1,0:T(8,128)S(1)}, u32[]{:S(2)}, u32[]{:S(2)}) collective-permute-start(f32[8,128,128]{2,1,0:T(8,128)S(1)} %multiply_add_fusion.2), channel_id=1, source_target_pairs={{0,4},{4,8},{8,12},{12,16},{16,20},{20,24},{24,28},{28,32},{32,36}... | collective-permute-start | bytes 1572872 | tf_op jit(solution)/shard_map/while/body/eval_jaxpr/ppermute | solution.py:14
  569.1 12.6 %collective-permute-start = (f32[8,128,128]{2,1,0:T(8,128)S(1)}, f32[8,128,128]{2,1,0:T(8,128)S(1)}, u32[]{:S(2)}, u32[]{:S(2)}) collective-permute-start(f32[8,128,128]{2,1,0:T(8,128)S(1)} %multiply_add_fusion.2), channel_id=1, source_target_pairs={{0,4},{4,8},{8,12},{12,16},{16,20},{20,24},{24,28},{28,32},{32,36}... | collective-permute-start | bytes 1572872 | tf_op jit(solution)/shard_map/while/body/eval_jaxpr/ppermute | solution.py:14
  582.9 12.6 %collective-permute-start = (f32[8,128,128]{2,1,0:T(8,128)S(1)}, f32[8,128,128]{2,1,0:T(8,128)S(1)}, u32[]{:S(2)}, u32[]{:S(2)}) collective-permute-start(f32[8,128,128]{2,1,0:T(8,128)S(1)} %multiply_add_fusion.2), channel_id=1, source_target_pairs={{0,4},{4,8},{8,12},{12,16},{16,20},{20,24},{24,28},{28,32},{32,36}... | collective-permute-start | bytes 1572872 | tf_op jit(solution)/shard_map/while/body/eval_jaxpr/ppermute | solution.py:14
  596.7 12.6 %collective-permute-start = (f32[8,128,128]{2,1,0:T(8,128)S(1)}, f32[8,128,128]{2,1,0:T(8,128)S(1)}, u32[]{:S(2)}, u32[]{:S(2)}) collective-permute-start(f32[8,128,128]{2,1,0:T(8,128)S(1)} %multiply_add_fusion.2), channel_id=1, source_target_pairs={{0,4},{4,8},{8,12},{12,16},{16,20},{20,24},{24,28},{28,32},{32,36}... | collective-permute-start | bytes 1572872 | tf_op jit(solution)/shard_map/while/body/eval_jaxpr/ppermute | solution.py:14
  610.4 12.6 %collective-permute-start = (f32[8,128,128]{2,1,0:T(8,128)S(1)}, f32[8,128,128]{2,1,0:T(8,128)S(1)}, u32[]{:S(2)}, u32[]{:S(2)}) collective-permute-start(f32[8,128,128]{2,1,0:T(8,128)S(1)} %multiply_add_fusion.2), channel_id=1, source_target_pairs={{0,4},{4,8},{8,12},{12,16},{16,20},{20,24},{24,28},{28,32},{32,36}... | collective-permute-start | bytes 1572872 | tf_op jit(solution)/shard_map/while/body/eval_jaxpr/ppermute | solution.py:14
  624.2 12.6 %collective-permute-start = (f32[8,128,128]{2,1,0:T(8,128)S(1)}, f32[8,128,128]{2,1,0:T(8,128)S(1)}, u32[]{:S(2)}, u32[]{:S(2)}) collective-permute-start(f32[8,128,128]{2,1,0:T(8,128)S(1)} %multiply_add_fusion.2), channel_id=1, source_target_pairs={{0,4},{4,8},{8,12},{12,16},{16,20},{20,24},{24,28},{28,32},{32,36}... | collective-permute-start | bytes 1572872 | tf_op jit(solution)/shard_map/while/body/eval_jaxpr/ppermute | solution.py:14
  638.0 12.6 %collective-permute-start = (f32[8,128,128]{2,1,0:T(8,128)S(1)}, f32[8,128,128]{2,1,0:T(8,128)S(1)}, u32[]{:S(2)}, u32[]{:S(2)}) collective-permute-start(f32[8,128,128]{2,1,0:T(8,128)S(1)} %multiply_add_fusion.2), channel_id=1, source_target_pairs={{0,4},{4,8},{8,12},{12,16},{16,20},{20,24},{24,28},{28,32},{32,36}... | collective-permute-start | bytes 1572872 | tf_op jit(solution)/shard_map/while/body/eval_jaxpr/ppermute | solution.py:14
  651.8 12.6 %collective-permute-start = (f32[8,128,128]{2,1,0:T(8,128)S(1)}, f32[8,128,128]{2,1,0:T(8,128)S(1)}, u32[]{:S(2)}, u32[]{:S(2)}) collective-permute-start(f32[8,128,128]{2,1,0:T(8,128)S(1)} %multiply_add_fusion.2), channel_id=1, source_target_pairs={{0,4},{4,8},{8,12},{12,16},{16,20},{20,24},{24,28},{28,32},{32,36}... | collective-permute-start | bytes 1572872 | tf_op jit(solution)/shard_map/while/body/eval_jaxpr/ppermute | solution.py:14
  (26 other events, 589.2 us)
Sparse Core Ops, SparseCore 0:
  665.5 112.1 all-gather.1
where the time goes:
time: 808 us; the launch traced here: 801 us
  waiting for transfers between devices  255 us (32%)
  local copies, waits for them, and re-layouts  231 us (29%)
  starting transfers between devices  163 us (20%)
  matrix products  75.3 us (9%)
  other arithmetic  52.4 us (6%)
  between operations  14.2 us (2%)
  blocking collectives  9.83 us (1%)
    ppermute x31, waiting for transfers between devices, from_behind(): lax.ppermute(value, axis, [(source, source + steps) for source in range(f...  189 us
    dynamic_update_slice x8, local copies, waits for them, and re-layouts, shards(): lax.scan(local_step, zero_state, (query_blocks, key_blocks, value_blocks,...  178 us
    ppermute x31, starting transfers between devices, from_behind(): lax.ppermute(value, axis, [(source, source + steps) for source in range(f...  163 us
    all_gather x1, waiting for transfers between devices, shards(): lax.all_gather(snapshots, 'seq', axis=0, tiled=True)  65.4 us
    add x31, other arithmetic, combine(): jnp.exp(following[0])[:, None, None] * earlier[1] + following[1]  36.1 us
    dot_general x4, matrix products, block_terms(): jnp.einsum('hts,shd->thd', weights, value_blk, preferred_element_type=jnp...  20.8 us
    unnamed x25, local copies, waits for them, and re-layouts  20.6 us
  transfers between devices with their start and end apart: 32, of which 32 were waited for; matrix products, arithmetic and copies ran while one was open for 5% of the time, Pallas kernels for 0%

commit v1 on v0

--- a/solution.py
+++ b/solution.py
@@ -107,7 +107,9 @@
     gathered = jnp.einsum(
         "sn,nhde->shde",
         chosen.astype(jnp.bfloat16),
-        lax.all_gather(snapshots, "seq", axis=0, tiled=True),
+        jnp.concatenate(
+            lax.all_to_all(jnp.stack([snapshots] * lax.axis_size("seq")), "seq", 0, 0), axis=0
+        ),
         preferred_element_type=jnp.float32,
     )
     page_cache = gathered.astype(jnp.bfloat16)

time: 808 us -> 1020 us (1.26)
  the two profiles are of different devices: /device:TPU:1 before, /device:TPU:44 now
where the time goes in v1:
time: 1020 us; the launch traced here: 1010 us
  waiting for transfers between devices  541 us (53%)
  local copies, waits for them, and re-layouts  271 us (27%)
  starting transfers between devices  77.2 us (8%)
  matrix products  59.4 us (6%)
  other arithmetic  52.1 us (5%)
    ppermute x31, waiting for transfers between devices, from_behind(): lax.ppermute(value, axis, [(source, source + steps) for source in range(f...  318 us
    all_to_all x1, waiting for transfers between devices, shards(): lax.all_to_all(jnp.stack([snapshots] * lax.axis_size('seq')), 'seq', 0, 0)  223 us
    dynamic_update_slice x8, local copies, waits for them, and re-layouts, shards(): lax.scan(local_step, zero_state, (query_blocks, key_blocks, value_blocks,...  172 us
    ppermute x31, starting transfers between devices, from_behind(): lax.ppermute(value, axis, [(source, source + steps) for source in range(f...  59.5 us
    add x31, other arithmetic, combine(): jnp.exp(following[0])[:, None, None] * earlier[1] + following[1]  36.1 us
    dot_general x4, matrix products, block_terms(): jnp.einsum('hts,shd->thd', weights, value_blk, preferred_element_type=jnp...  21.3 us
    unnamed x25, local copies, waits for them, and re-layouts  20.6 us
  transfers between devices with their start and end apart: 32, of which 32 were waited for; matrix products, arithmetic and copies ran while one was open for 4% of the time, Pallas kernels for 0%

profile of v1, /device:TPU:44, one launch (start us, length us, event | category | flops | bytes accessed | tf_op | source)
XLA Modules:
  0.0 1011.6 jit_solution(1947246291215279731)
XLA Ops:
  20.5 248.6 %while.28 = (s32[]{:T(128)}, f32[8,128,128]{2,1,0:T(8,128)}, f32[4,512,8,128]{1,0,3,2:T(4,128)}, f32[4,8,128,128]{3,2,1,0:T(8,128)}, f32[4,8,512]{2,1,0:T(8,128)...) while((s32[]{:T(128)}, f32[8,128,128]{2,1,0:T(8,128)}, ...), condition=%wide.region_3.4_spmd.clone, body=%wide.region_2.3_spmd.clone.sunk | while | flops 2027163648 | bytes 34407320 | solution.py:64
  36.3 40.8 %dynamic_update_slice.14 = f32[4,512,8,128]{1,0,3,2:T(4,128)} dynamic-update-slice(f32[4,512,8,128]{1,0,3,2:T(4,128)} %get-tuple-element.309, f32[1,512,8,128]{1,0,3,2:T(1,128)S(1)} %copy.183, s32[]{:T(128)} %get-tuple-element.307, s32[]{:T(128)} %constant.44.clone.1..sunk, s32[]{:T(128)} %constant.44.clone.1..sunk, s32[]{:T(128)} %constant.44.clone.1..sunk) | dynamic-update-slice | bytes 4194308 | tf_op jit(solution)/shard_map/while/body/jit(dynamic_update_index_in_dim)/dynamic_update_slice | solution.py:64
  98.8 40.8 %dynamic_update_slice.14 = f32[4,512,8,128]{1,0,3,2:T(4,128)} dynamic-update-slice(f32[4,512,8,128]{1,0,3,2:T(4,128)} %get-tuple-element.309, f32[1,512,8,128]{1,0,3,2:T(1,128)S(1)} %copy.183, s32[]{:T(128)} %get-tuple-element.307, s32[]{:T(128)} %constant.44.clone.1..sunk, s32[]{:T(128)} %constant.44.clone.1..sunk, s32[]{:T(128)} %constant.44.clone.1..sunk) | dynamic-update-slice | bytes 4194308 | tf_op jit(solution)/shard_map/while/body/jit(dynamic_update_index_in_dim)/dynamic_update_slice | solution.py:64
  161.2 40.8 %dynamic_update_slice.14 = f32[4,512,8,128]{1,0,3,2:T(4,128)} dynamic-update-slice(f32[4,512,8,128]{1,0,3,2:T(4,128)} %get-tuple-element.309, f32[1,512,8,128]{1,0,3,2:T(1,128)S(1)} %copy.183, s32[]{:T(128)} %get-tuple-element.307, s32[]{:T(128)} %constant.44.clone.1..sunk, s32[]{:T(128)} %constant.44.clone.1..sunk, s32[]{:T(128)} %constant.44.clone.1..sunk) | dynamic-update-slice | bytes 4194308 | tf_op jit(solution)/shard_map/while/body/jit(dynamic_update_index_in_dim)/dynamic_update_slice | solution.py:64
  223.6 40.8 %dynamic_update_slice.14 = f32[4,512,8,128]{1,0,3,2:T(4,128)} dynamic-update-slice(f32[4,512,8,128]{1,0,3,2:T(4,128)} %get-tuple-element.309, f32[1,512,8,128]{1,0,3,2:T(1,128)S(1)} %copy.183, s32[]{:T(128)} %get-tuple-element.307, s32[]{:T(128)} %constant.44.clone.1..sunk, s32[]{:T(128)} %constant.44.clone.1..sunk, s32[]{:T(128)} %constant.44.clone.1..sunk) | dynamic-update-slice | bytes 4194308 | tf_op jit(solution)/shard_map/while/body/jit(dynamic_update_index_in_dim)/dynamic_update_slice | solution.py:64
  269.8 414.6 %while.27 = (s32[]{:T(128)}, f32[8,128,128]{2,1,0:T(8,128)S(1)}, f32[8,1,1]{0,2,1:T(1,128)}, f32[8,128,128]{2,1,0:T(8,128)}, s32[]{:T(128)}) while((s32[]{:T(128)}, f32[8,128,128]{2,1,0:T(8,128)S(1)}, f32[8,1,1]{0,2,1:T(1,128)}, f32[8,128,128]{2,1,0:T(8,128)}, s32[]{:T(128)}) %tuple.70), condition=%wide.region_6.7_spmd, body=%wide.region_5.6_spmd.sunk | while | flops 262146 | bytes 3670149 | solution.py:75
  343.2 10.7 %collective-permute-done = f32[8,128,128]{2,1,0:T(8,128)S(1)} collective-permute-done((f32[8,128,128]{2,1,0:T(8,128)S(1)}, f32[8,128,128]{2,1,0:T(8,128)S(1)}, u32[]{:S(2)}, u32[]{:S(2)}) %collective-permute-start) | collective-permute-done | bytes 524320 | tf_op jit(solution)/shard_map/while/body/eval_jaxpr/ppermute | solution.py:14
  356.9 10.7 %collective-permute-done = f32[8,128,128]{2,1,0:T(8,128)S(1)} collective-permute-done((f32[8,128,128]{2,1,0:T(8,128)S(1)}, f32[8,128,128]{2,1,0:T(8,128)S(1)}, u32[]{:S(2)}, u32[]{:S(2)}) %collective-permute-start) | collective-permute-done | bytes 524320 | tf_op jit(solution)/shard_map/while/body/eval_jaxpr/ppermute | solution.py:14
  384.5 10.7 %collective-permute-done = f32[8,128,128]{2,1,0:T(8,128)S(1)} collective-permute-done((f32[8,128,128]{2,1,0:T(8,128)S(1)}, f32[8,128,128]{2,1,0:T(8,128)S(1)}, u32[]{:S(2)}, u32[]{:S(2)}) %collective-permute-start) | collective-permute-done | bytes 524320 | tf_op jit(solution)/shard_map/while/body/eval_jaxpr/ppermute | solution.py:14
  398.3 10.7 %collective-permute-done = f32[8,128,128]{2,1,0:T(8,128)S(1)} collective-permute-done((f32[8,128,128]{2,1,0:T(8,128)S(1)}, f32[8,128,128]{2,1,0:T(8,128)S(1)}, u32[]{:S(2)}, u32[]{:S(2)}) %collective-permute-start) | collective-permute-done | bytes 524320 | tf_op jit(solution)/shard_map/while/body/eval_jaxpr/ppermute | solution.py:14
  453.3 10.7 %collective-permute-done = f32[8,128,128]{2,1,0:T(8,128)S(1)} collective-permute-done((f32[8,128,128]{2,1,0:T(8,128)S(1)}, f32[8,128,128]{2,1,0:T(8,128)S(1)}, u32[]{:S(2)}, u32[]{:S(2)}) %collective-permute-start) | collective-permute-done | bytes 524320 | tf_op jit(solution)/shard_map/while/body/eval_jaxpr/ppermute | solution.py:14
  467.1 10.7 %collective-permute-done = f32[8,128,128]{2,1,0:T(8,128)S(1)} collective-permute-done((f32[8,128,128]{2,1,0:T(8,128)S(1)}, f32[8,128,128]{2,1,0:T(8,128)S(1)}, u32[]{:S(2)}, u32[]{:S(2)}) %collective-permute-start) | collective-permute-done | bytes 524320 | tf_op jit(solution)/shard_map/while/body/eval_jaxpr/ppermute | solution.py:14
  522.2 10.7 %collective-permute-done = f32[8,128,128]{2,1,0:T(8,128)S(1)} collective-permute-done((f32[8,128,128]{2,1,0:T(8,128)S(1)}, f32[8,128,128]{2,1,0:T(8,128)S(1)}, u32[]{:S(2)}, u32[]{:S(2)}) %collective-permute-start) | collective-permute-done | bytes 524320 | tf_op jit(solution)/shard_map/while/body/eval_jaxpr/ppermute | solution.py:14
  536.0 10.7 %collective-permute-done = f32[8,128,128]{2,1,0:T(8,128)S(1)} collective-permute-done((f32[8,128,128]{2,1,0:T(8,128)S(1)}, f32[8,128,128]{2,1,0:T(8,128)S(1)}, u32[]{:S(2)}, u32[]{:S(2)}) %collective-permute-start) | collective-permute-done | bytes 524320 | tf_op jit(solution)/shard_map/while/body/eval_jaxpr/ppermute | solution.py:14
  591.1 10.7 %collective-permute-done = f32[8,128,128]{2,1,0:T(8,128)S(1)} collective-permute-done((f32[8,128,128]{2,1,0:T(8,128)S(1)}, f32[8,128,128]{2,1,0:T(8,128)S(1)}, u32[]{:S(2)}, u32[]{:S(2)}) %collective-permute-start) | collective-permute-done | bytes 524320 | tf_op jit(solution)/shard_map/while/body/eval_jaxpr/ppermute | solution.py:14
  604.9 10.7 %collective-permute-done = f32[8,128,128]{2,1,0:T(8,128)S(1)} collective-permute-done((f32[8,128,128]{2,1,0:T(8,128)S(1)}, f32[8,128,128]{2,1,0:T(8,128)S(1)}, u32[]{:S(2)}, u32[]{:S(2)}) %collective-permute-start) | collective-permute-done | bytes 524320 | tf_op jit(solution)/shard_map/while/body/eval_jaxpr/ppermute | solution.py:14
  646.2 10.7 %collective-permute-done = f32[8,128,128]{2,1,0:T(8,128)S(1)} collective-permute-done((f32[8,128,128]{2,1,0:T(8,128)S(1)}, f32[8,128,128]{2,1,0:T(8,128)S(1)}, u32[]{:S(2)}, u32[]{:S(2)}) %collective-permute-start) | collective-permute-done | bytes 524320 | tf_op jit(solution)/shard_map/while/body/eval_jaxpr/ppermute | solution.py:14
  660.0 10.7 %collective-permute-done = f32[8,128,128]{2,1,0:T(8,128)S(1)} collective-permute-done((f32[8,128,128]{2,1,0:T(8,128)S(1)}, f32[8,128,128]{2,1,0:T(8,128)S(1)}, u32[]{:S(2)}, u32[]{:S(2)}) %collective-permute-start) | collective-permute-done | bytes 524320 | tf_op jit(solution)/shard_map/while/body/eval_jaxpr/ppermute | solution.py:14
  685.2 16.5 %stack.2 = bf16[32,2,8,128,128]{4,1,3,2,0:T(2,128)(2,1)} broadcast(bf16[2,8,128,128]{3,0,2,1:T(2,128)(2,1)S(1)} %copy.113), dimensions={1,2,3,4} | broadcast | bytes 17301504 | tf_op jit(solution)/shard_map/stack | solution.py:111
  701.6 17.6 %all-to-all-start = ((bf16[32,2,8,128,128]{4,1,3,2,0:T(2,128)(2,1)}), bf16[32,2,8,128,128]{4,1,3,2,0:T(2,128)(2,1)}, u32[]{:S(2)}, u32[]{:S(2)}) async-start(bf16[32,2,8,128,128]{4,1,3,2,0:T(2,128)(2,1)} %stack.2), calls=%async_computation | async-start | bytes 33554432 | tf_op jit(solution)/shard_map/all_to_all | solution.py:111
  719.5 10.9 %reshape.97 = f32[2048,8,128]{0,2,1:T(8,128)} reshape(f32[4,512,8,128]{1,0,3,2:T(4,128)} %get-tuple-element.96) | data formatting | bytes 16777216 | tf_op jit(solution)/shard_map/reshape | solution.py:86
  731.3 12.3 %multiply_reduce_fusion = (f32[2048]{0:T(1024)S(1)}, f32[2048,8,128]{0,2,1:T(8,128)}) fusion(f32[2048,8,128]{0,2,1:T(8,128)} %reshape.97, f32[2048,8]{0,1:T(8,128)S(1)} %exponential_bitcast_fusion.2, f32[8,128,128]{2,1,0:T(8,128)S(1)} %get-tuple-element.98, bf16[2048,1024]{1,0:T(8,128)(2,1)} %param.10), kind=kOutput, calls=%fused_computation.32 | convolution fusion | flops 3229612032 | bytes 21569536 | tf_op jit(solution)/shard_map/thd,hde->the/dot_general | solution.py:79
  765.6 223.0 %all-to-all-done = bf16[32,2,8,128,128]{4,1,3,2,0:T(2,128)(2,1)} async-done(((bf16[32,2,8,128,128]{4,1,3,2,0:T(2,128)(2,1)}), bf16[32,2,8,128,128]{4,1,3,2,0:T(2,128)(2,1)}, u32[]{:S(2)}, u32[]{:S(2)}) %all-to-all-start) | async-done | bytes 16777248 | tf_op jit(solution)/shard_map/all_to_all | solution.py:111
  988.6 19.2 %copy.114 = bf16[32,2,8,128,128]{4,1,0,3,2:T(2,128)(2,1)S(1)} copy(bf16[32,2,8,128,128]{4,1,3,2,0:T(2,128)(2,1)} %all-to-all-done) | data formatting | bytes 33554432 | tf_op jit(solution)/shard_map/all_to_all | solution.py:111
  (221 shorter events, 419.1 us)
Async XLA Ops:
  341.2 12.6 %collective-permute-start = (f32[8,128,128]{2,1,0:T(8,128)S(1)}, f32[8,128,128]{2,1,0:T(8,128)S(1)}, u32[]{:S(2)}, u32[]{:S(2)}) collective-permute-start(f32[8,128,128]{2,1,0:T(8,128)S(1)} %multiply_add_fusion.2), channel_id=1, source_target_pairs={{0,4},{4,8},{8,12},{12,16},{16,20},{20,24},{24,28},{28,32},{32,36}... | collective-permute-start | bytes 1572872 | tf_op jit(solution)/shard_map/while/body/eval_jaxpr/ppermute | solution.py:14
  355.0 12.6 %collective-permute-start = (f32[8,128,128]{2,1,0:T(8,128)S(1)}, f32[8,128,128]{2,1,0:T(8,128)S(1)}, u32[]{:S(2)}, u32[]{:S(2)}) collective-permute-start(f32[8,128,128]{2,1,0:T(8,128)S(1)} %multiply_add_fusion.2), channel_id=1, source_target_pairs={{0,4},{4,8},{8,12},{12,16},{16,20},{20,24},{24,28},{28,32},{32,36}... | collective-permute-start | bytes 1572872 | tf_op jit(solution)/shard_map/while/body/eval_jaxpr/ppermute | solution.py:14
  368.8 12.6 %collective-permute-start = (f32[8,128,128]{2,1,0:T(8,128)S(1)}, f32[8,128,128]{2,1,0:T(8,128)S(1)}, u32[]{:S(2)}, u32[]{:S(2)}) collective-permute-start(f32[8,128,128]{2,1,0:T(8,128)S(1)} %multiply_add_fusion.2), channel_id=1, source_target_pairs={{0,4},{4,8},{8,12},{12,16},{16,20},{20,24},{24,28},{28,32},{32,36}... | collective-permute-start | bytes 1572872 | tf_op jit(solution)/shard_map/while/body/eval_jaxpr/ppermute | solution.py:14
  382.5 12.6 %collective-permute-start = (f32[8,128,128]{2,1,0:T(8,128)S(1)}, f32[8,128,128]{2,1,0:T(8,128)S(1)}, u32[]{:S(2)}, u32[]{:S(2)}) collective-permute-start(f32[8,128,128]{2,1,0:T(8,128)S(1)} %multiply_add_fusion.2), channel_id=1, source_target_pairs={{0,4},{4,8},{8,12},{12,16},{16,20},{20,24},{24,28},{28,32},{32,36}... | collective-permute-start | bytes 1572872 | tf_op jit(solution)/shard_map/while/body/eval_jaxpr/ppermute | solution.py:14
  396.3 12.6 %collective-permute-start = (f32[8,128,128]{2,1,0:T(8,128)S(1)}, f32[8,128,128]{2,1,0:T(8,128)S(1)}, u32[]{:S(2)}, u32[]{:S(2)}) collective-permute-start(f32[8,128,128]{2,1,0:T(8,128)S(1)} %multiply_add_fusion.2), channel_id=1, source_target_pairs={{0,4},{4,8},{8,12},{12,16},{16,20},{20,24},{24,28},{28,32},{32,36}... | collective-permute-start | bytes 1572872 | tf_op jit(solution)/shard_map/while/body/eval_jaxpr/ppermute | solution.py:14
  410.1 12.6 %collective-permute-start = (f32[8,128,128]{2,1,0:T(8,128)S(1)}, f32[8,128,128]{2,1,0:T(8,128)S(1)}, u32[]{:S(2)}, u32[]{:S(2)}) collective-permute-start(f32[8,128,128]{2,1,0:T(8,128)S(1)} %multiply_add_fusion.2), channel_id=1, source_target_pairs={{0,4},{4,8},{8,12},{12,16},{16,20},{20,24},{24,28},{28,32},{32,36}... | collective-permute-start | bytes 1572872 | tf_op jit(solution)/shard_map/while/body/eval_jaxpr/ppermute | solution.py:14
  423.9 12.6 %collective-permute-start = (f32[8,128,128]{2,1,0:T(8,128)S(1)}, f32[8,128,128]{2,1,0:T(8,128)S(1)}, u32[]{:S(2)}, u32[]{:S(2)}) collective-permute-start(f32[8,128,128]{2,1,0:T(8,128)S(1)} %multiply_add_fusion.2), channel_id=1, source_target_pairs={{0,4},{4,8},{8,12},{12,16},{16,20},{20,24},{24,28},{28,32},{32,36}... | collective-permute-start | bytes 1572872 | tf_op jit(solution)/shard_map/while/body/eval_jaxpr/ppermute | solution.py:14
  437.6 12.6 %collective-permute-start = (f32[8,128,128]{2,1,0:T(8,128)S(1)}, f32[8,128,128]{2,1,0:T(8,128)S(1)}, u32[]{:S(2)}, u32[]{:S(2)}) collective-permute-start(f32[8,128,128]{2,1,0:T(8,128)S(1)} %multiply_add_fusion.2), channel_id=1, source_target_pairs={{0,4},{4,8},{8,12},{12,16},{16,20},{20,24},{24,28},{28,32},{32,36}... | collective-permute-start | bytes 1572872 | tf_op jit(solution)/shard_map/while/body/eval_jaxpr/ppermute | solution.py:14
  451.4 12.6 %collective-permute-start = (f32[8,128,128]{2,1,0:T(8,128)S(1)}, f32[8,128,128]{2,1,0:T(8,128)S(1)}, u32[]{:S(2)}, u32[]{:S(2)}) collective-permute-start(f32[8,128,128]{2,1,0:T(8,128)S(1)} %multiply_add_fusion.2), channel_id=1, source_target_pairs={{0,4},{4,8},{8,12},{12,16},{16,20},{20,24},{24,28},{28,32},{32,36}... | collective-permute-start | bytes 1572872 | tf_op jit(solution)/shard_map/while/body/eval_jaxpr/ppermute | solution.py:14
  465.2 12.6 %collective-permute-start = (f32[8,128,128]{2,1,0:T(8,128)S(1)}, f32[8,128,128]{2,1,0:T(8,128)S(1)}, u32[]{:S(2)}, u32[]{:S(2)}) collective-permute-start(f32[8,128,128]{2,1,0:T(8,128)S(1)} %multiply_add_fusion.2), channel_id=1, source_target_pairs={{0,4},{4,8},{8,12},{12,16},{16,20},{20,24},{24,28},{28,32},{32,36}... | collective-permute-start | bytes 1572872 | tf_op jit(solution)/shard_map/while/body/eval_jaxpr/ppermute | solution.py:14
  479.0 12.6 %collective-permute-start = (f32[8,128,128]{2,1,0:T(8,128)S(1)}, f32[8,128,128]{2,1,0:T(8,128)S(1)}, u32[]{:S(2)}, u32[]{:S(2)}) collective-permute-start(f32[8,128,128]{2,1,0:T(8,128)S(1)} %multiply_add_fusion.2), channel_id=1, source_target_pairs={{0,4},{4,8},{8,12},{12,16},{16,20},{20,24},{24,28},{28,32},{32,36}... | collective-permute-start | bytes 1572872 | tf_op jit(solution)/shard_map/while/body/eval_jaxpr/ppermute | solution.py:14
  492.7 12.6 %collective-permute-start = (f32[8,128,128]{2,1,0:T(8,128)S(1)}, f32[8,128,128]{2,1,0:T(8,128)S(1)}, u32[]{:S(2)}, u32[]{:S(2)}) collective-permute-start(f32[8,128,128]{2,1,0:T(8,128)S(1)} %multiply_add_fusion.2), channel_id=1, source_target_pairs={{0,4},{4,8},{8,12},{12,16},{16,20},{20,24},{24,28},{28,32},{32,36}... | collective-permute-start | bytes 1572872 | tf_op jit(solution)/shard_map/while/body/eval_jaxpr/ppermute | solution.py:14
  506.5 12.6 %collective-permute-start = (f32[8,128,128]{2,1,0:T(8,128)S(1)}, f32[8,128,128]{2,1,0:T(8,128)S(1)}, u32[]{:S(2)}, u32[]{:S(2)}) collective-permute-start(f32[8,128,128]{2,1,0:T(8,128)S(1)} %multiply_add_fusion.2), channel_id=1, source_target_pairs={{0,4},{4,8},{8,12},{12,16},{16,20},{20,24},{24,28},{28,32},{32,36}... | collective-permute-start | bytes 1572872 | tf_op jit(solution)/shard_map/while/body/eval_jaxpr/ppermute | solution.py:14
  520.3 12.6 %collective-permute-start = (f32[8,128,128]{2,1,0:T(8,128)S(1)}, f32[8,128,128]{2,1,0:T(8,128)S(1)}, u32[]{:S(2)}, u32[]{:S(2)}) collective-permute-start(f32[8,128,128]{2,1,0:T(8,128)S(1)} %multiply_add_fusion.2), channel_id=1, source_target_pairs={{0,4},{4,8},{8,12},{12,16},{16,20},{20,24},{24,28},{28,32},{32,36}... | collective-permute-start | bytes 1572872 | tf_op jit(solution)/shard_map/while/body/eval_jaxpr/ppermute | solution.py:14
  534.1 12.6 %collective-permute-start = (f32[8,128,128]{2,1,0:T(8,128)S(1)}, f32[8,128,128]{2,1,0:T(8,128)S(1)}, u32[]{:S(2)}, u32[]{:S(2)}) collective-permute-start(f32[8,128,128]{2,1,0:T(8,128)S(1)} %multiply_add_fusion.2), channel_id=1, source_target_pairs={{0,4},{4,8},{8,12},{12,16},{16,20},{20,24},{24,28},{28,32},{32,36}... | collective-permute-start | bytes 1572872 | tf_op jit(solution)/shard_map/while/body/eval_jaxpr/ppermute | solution.py:14
  547.8 12.6 %collective-permute-start = (f32[8,128,128]{2,1,0:T(8,128)S(1)}, f32[8,128,128]{2,1,0:T(8,128)S(1)}, u32[]{:S(2)}, u32[]{:S(2)}) collective-permute-start(f32[8,128,128]{2,1,0:T(8,128)S(1)} %multiply_add_fusion.2), channel_id=1, source_target_pairs={{0,4},{4,8},{8,12},{12,16},{16,20},{20,24},{24,28},{28,32},{32,36}... | collective-permute-start | bytes 1572872 | tf_op jit(solution)/shard_map/while/body/eval_jaxpr/ppermute | solution.py:14
  561.6 12.6 %collective-permute-start = (f32[8,128,128]{2,1,0:T(8,128)S(1)}, f32[8,128,128]{2,1,0:T(8,128)S(1)}, u32[]{:S(2)}, u32[]{:S(2)}) collective-permute-start(f32[8,128,128]{2,1,0:T(8,128)S(1)} %multiply_add_fusion.2), channel_id=1, source_target_pairs={{0,4},{4,8},{8,12},{12,16},{16,20},{20,24},{24,28},{28,32},{32,36}... | collective-permute-start | bytes 1572872 | tf_op jit(solution)/shard_map/while/body/eval_jaxpr/ppermute | solution.py:14
  589.2 12.6 %collective-permute-start = (f32[8,128,128]{2,1,0:T(8,128)S(1)}, f32[8,128,128]{2,1,0:T(8,128)S(1)}, u32[]{:S(2)}, u32[]{:S(2)}) collective-permute-start(f32[8,128,128]{2,1,0:T(8,128)S(1)} %multiply_add_fusion.2), channel_id=1, source_target_pairs={{0,4},{4,8},{8,12},{12,16},{16,20},{20,24},{24,28},{28,32},{32,36}... | collective-permute-start | bytes 1572872 | tf_op jit(solution)/shard_map/while/body/eval_jaxpr/ppermute | solution.py:14
  602.9 12.6 %collective-permute-start = (f32[8,128,128]{2,1,0:T(8,128)S(1)}, f32[8,128,128]{2,1,0:T(8,128)S(1)}, u32[]{:S(2)}, u32[]{:S(2)}) collective-permute-start(f32[8,128,128]{2,1,0:T(8,128)S(1)} %multiply_add_fusion.2), channel_id=1, source_target_pairs={{0,4},{4,8},{8,12},{12,16},{16,20},{20,24},{24,28},{28,32},{32,36}... | collective-permute-start | bytes 1572872 | tf_op jit(solution)/shard_map/while/body/eval_jaxpr/ppermute | solution.py:14
  616.7 12.6 %collective-permute-start = (f32[8,128,128]{2,1,0:T(8,128)S(1)}, f32[8,128,128]{2,1,0:T(8,128)S(1)}, u32[]{:S(2)}, u32[]{:S(2)}) collective-permute-start(f32[8,128,128]{2,1,0:T(8,128)S(1)} %multiply_add_fusion.2), channel_id=1, source_target_pairs={{0,4},{4,8},{8,12},{12,16},{16,20},{20,24},{24,28},{28,32},{32,36}... | collective-permute-start | bytes 1572872 | tf_op jit(solution)/shard_map/while/body/eval_jaxpr/ppermute | solution.py:14
  644.2 12.6 %collective-permute-start = (f32[8,128,128]{2,1,0:T(8,128)S(1)}, f32[8,128,128]{2,1,0:T(8,128)S(1)}, u32[]{:S(2)}, u32[]{:S(2)}) collective-permute-start(f32[8,128,128]{2,1,0:T(8,128)S(1)} %multiply_add_fusion.2), channel_id=1, source_target_pairs={{0,4},{4,8},{8,12},{12,16},{16,20},{20,24},{24,28},{28,32},{32,36}... | collective-permute-start | bytes 1572872 | tf_op jit(solution)/shard_map/while/body/eval_jaxpr/ppermute | solution.py:14
  658.0 12.6 %collective-permute-start = (f32[8,128,128]{2,1,0:T(8,128)S(1)}, f32[8,128,128]{2,1,0:T(8,128)S(1)}, u32[]{:S(2)}, u32[]{:S(2)}) collective-permute-start(f32[8,128,128]{2,1,0:T(8,128)S(1)} %multiply_add_fusion.2), channel_id=1, source_target_pairs={{0,4},{4,8},{8,12},{12,16},{16,20},{20,24},{24,28},{28,32},{32,36}... | collective-permute-start | bytes 1572872 | tf_op jit(solution)/shard_map/while/body/eval_jaxpr/ppermute | solution.py:14
  671.8 12.6 %collective-permute-start = (f32[8,128,128]{2,1,0:T(8,128)S(1)}, f32[8,128,128]{2,1,0:T(8,128)S(1)}, u32[]{:S(2)}, u32[]{:S(2)}) collective-permute-start(f32[8,128,128]{2,1,0:T(8,128)S(1)} %multiply_add_fusion.2), channel_id=1, source_target_pairs={{0,4},{4,8},{8,12},{12,16},{16,20},{20,24},{24,28},{28,32},{32,36}... | collective-permute-start | bytes 1572872 | tf_op jit(solution)/shard_map/while/body/eval_jaxpr/ppermute | solution.py:14
  701.6 287.0 %all-to-all-start = ((bf16[32,2,8,128,128]{4,1,3,2,0:T(2,128)(2,1)}), bf16[32,2,8,128,128]{4,1,3,2,0:T(2,128)(2,1)}, u32[]{:S(2)}, u32[]{:S(2)}) async-start(bf16[32,2,8,128,128]{4,1,3,2,0:T(2,128)(2,1)} %stack.2), calls=%async_computation | async-start | bytes 33554432 | tf_op jit(solution)/shard_map/all_to_all | solution.py:111
  (30 other events, 930.0 us)
